TPU v7x, 32 devices: a whole 2x2x4 slice. The times are simulated.
32 devices in a mesh: domain: 8 (over y, x, core), band: 4 (over z).
Axes of the slice: x: 2, y: 2, z: 4, core: 2. Of those that a mesh axis runs over, the one named last changes fastest.
Arguments:
- psi: float32 [4, 48, 32, 128], P('band', 'domain'), may hold values from -6 to 6
- potential: float32 [48, 32, 128], P('domain', 'band'), may hold values from -2 to 2
- projectors: float32 [8, 8, 2, 8, 1024], P('domain'), may hold values from -0.1875 to 0.1875
- offsets: int32 [8, 8, 2], P('domain'), may hold values from 0 to 184
- intersection: int32 [8, 8, 2], P('domain'), may hold values from -1 to 31, as said below
- dmat: float32 [256, 8, 8], P('domain'), may hold values from -9 to 9
Outputs:
- filtered: float32 [4, 48, 32, 128], P('band', 'domain')
Inputs may be any that keep to these rules, and one draw needn't show every extreme that they name: intersection[s, d, k] is -1 for an empty slot, else the index among the 32 atoms owned by domain device d of an atom whose projector reaches into domain device s's block; in every draw some owner d receives all 2 slots live from every source s. `offsets`: footprints are whole runs of 8 tiles inside the source block and may intersection one another.
All inputs are finite; a program needn't handle non-finite values.
Results may differ from a plain program's by a relative error of at most 0.00022.
Values sent between devices are 32-bit elements; how exact they have to be, the bound alone decides.
No kernel may reach another device: no remote copies, remote signals or barrier semaphores. Data moves between devices by JAX's collectives and lax.ppermute only.
A program may use at most 64 MiB of HBM per device.

v0:
```python
import jax
import jax.numpy as jnp
from jax import lax
from jax.sharding import PartitionSpec as P

DEGREE = 4
stencil_weights = (
    -5369.0 / 1800.0,
    12.0 / 7.0,
    -15.0 / 56.0,
    10.0 / 189.0,
    -1.0 / 112.0,
    2.0 / 1925.0,
    -1.0 / 16632.0,
)
filter_center = 6.0
filter_half_width = 4.0
highest = lax.Precision.HIGHEST


def extended(value, sides, width):
    for axis, dim in sides:
        size, length = (lax.axis_size(axis), value.shape[dim])
        up = [(i, (i + 1) % size) for i in range(size - 1)]
        down = [(j, i) for i, j in up]
        last = lax.slice_in_dim(value, length - width, length, axis=dim)
        initial = lax.slice_in_dim(value, 0, width, axis=dim)
        before = lax.ppermute(last, axis, up)
        after = lax.ppermute(initial, axis, down)
        value = jnp.concatenate([before, value, after], axis=dim)
    return value


def kinetic(grid_field, padded, reach_cells):
    planes = grid_field.shape[0]
    summed = 3.0 * stencil_weights[0] * grid_field
    for distance in range(1, reach_cells + 1):
        beside_all = (
            padded[reach_cells + distance : reach_cells + distance + planes]
            + padded[reach_cells - distance : reach_cells - distance + planes]
        )
        beside_all = (
            beside_all + jnp.roll(grid_field, distance, 1) + jnp.roll(grid_field, -distance, 1)
        )
        beside_all = (
            beside_all + jnp.roll(grid_field, distance, 2) + jnp.roll(grid_field, -distance, 2)
        )
        summed = summed + stencil_weights[distance] * beside_all
    return -0.5 * summed


def shards(psi, potential, projectors, offsets, intersection, dmat):
    reach_cells = len(stencil_weights) - 1
    pot_full = lax.all_gather(potential, "band", axis=1, tiled=True)
    projector_block = projectors[0]
    domains = projector_block.shape[0]
    cap_slots = projector_block.shape[1]
    proj_count = projector_block.shape[2]
    foot_tiles = projector_block.shape[3] // 128
    tile_index = (offsets[0][..., None] + jnp.arange(foot_tiles, dtype=jnp.int32)).reshape(-1)
    slot_atoms = intersection[0]
    live_slots = (slot_atoms >= 0).astype(jnp.float32)
    atom_count = dmat.shape[0]
    incoming = lax.all_to_all(slot_atoms, "domain", split_axis=0, concat_axis=0, tiled=True)
    in_hot = (incoming.reshape(-1)[:, None] == jnp.arange(atom_count, dtype=jnp.int32)).astype(
        jnp.float32
    )

    def owner_side(partial_value):
        received = lax.all_to_all(partial_value, "domain", split_axis=0, concat_axis=0, tiled=True)
        coefficient = jnp.dot(in_hot.T, received.reshape(-1, proj_count), precision=highest)
        applied = jnp.einsum("aij,aj->ai", dmat, coefficient, precision=highest)
        returned = jnp.dot(in_hot, applied, precision=highest).reshape(
            domains, cap_slots, proj_count
        )
        return lax.all_to_all(returned, "domain", split_axis=0, concat_axis=0, tiled=True)

    def hamiltonian(grid_field):
        padded = extended(grid_field, (("domain", 0),), reach_cells)
        tiles = grid_field.reshape(-1, 128)
        footprint = tiles[tile_index].reshape(domains, cap_slots, -1)
        partial_value = (
            jnp.einsum("dkil,dkl->dki", projector_block, footprint, precision=highest)
            * live_slots[..., None]
        )
        returned = owner_side(partial_value)
        contrib = jnp.einsum("dkil,dki->dkl", projector_block, returned, precision=highest).reshape(
            -1, 128
        )
        nonlocal_term = jnp.zeros_like(tiles).at[tile_index].add(contrib).reshape(grid_field.shape)
        return kinetic(grid_field, padded, reach_cells) + pot_full * grid_field + nonlocal_term

    state = psi[0]
    previous = state
    current = (hamiltonian(state) - filter_center * state) / filter_half_width
    for degree in range(1, DEGREE):
        following = (
            2.0 * (hamiltonian(current) - filter_center * current) / filter_half_width - previous
        )
        previous, current = (current, following)
    return current[None]


def solution(mesh):
    return jax.shard_map(
        shards,
        mesh=mesh,
        in_specs=(
            P("band", "domain", None, None),
            P("domain", "band", None),
            P("domain", None, None, None, None),
            P("domain", None, None),
            P("domain", None, None),
            P("domain", None, None),
        ),
        out_specs=P("band", "domain", None, None),
        check_vma=False,
    )
```

profile of v0, /device:TPU:0, one launch (start us, length us, event | category | flops | bytes accessed | tf_op | source)
XLA Modules:
  0.0 173.2 jit_solution(14876016404611144924)
XLA Ops:
  0.0 3.1 %collective-permute-start.1 = (f32[6,32,128]{2,1,0:T(8,128)}, f32[6,32,128]{2,1,0:T(8,128)}, u32[]{:S(2)}, u32[]{:S(2)}) collective-permute-start(f32[6,32,128]{2,1,0:T(8,128)} %bitcast.104), channel_id=1, source_target_pairs={{0,4},{4,8},{8,12},{12,16},{16,20},{20,24},{24,28},{1,5},{5,9},{9,... | collective-permute-start | bytes 294920 | tf_op jit(solution)/shard_map/ppermute | solution.py:28
  3.1 1.3 collective-permute-start
  4.4 1.3 copy.22
  5.8 6.5 %all-to-all-start = ((s32[8,1,2]{2,1,0:T(1,128)}), s32[8,1,2]{2,1,0:T(1,128)S(1)}, u32[]{:S(2)}, u32[]{:S(2)}) async-start(s32[8,1,2]{2,1,0:T(1,128)} %copy.22), calls=%async_computation | async-start | bytes 8192 | tf_op jit(solution)/shard_map/all_to_all | solution.py:64
  12.9 1.4 fusion.327
  14.3 1.4 fusion.331
  15.6 1.4 fusion.335
  25.1 1.1 fusion.14
  26.8 4.2 %all-to-all-start.1 = ((f32[8,2,8]{2,1,0:T(2,128)}), f32[8,2,8]{2,1,0:T(2,128)S(1)}, u32[]{:S(2)}, u32[]{:S(2)}) async-start(f32[8,2,8]{2,1,0:T(2,128)} %broadcast_multiply_fusion.4), calls=%async_computation.1 | async-start | bytes 16384 | tf_op jit(solution)/shard_map/all_to_all | solution.py:70
  32.8 2.9 %all-to-all-done.1 = f32[8,2,8]{2,1,0:T(2,128)S(1)} async-done(((f32[8,2,8]{2,1,0:T(2,128)}), f32[8,2,8]{2,1,0:T(2,128)S(1)}, u32[]{:S(2)}, u32[]{:S(2)}) %all-to-all-start.1) | async-done | bytes 544 | tf_op jit(solution)/shard_map/all_to_all | solution.py:70
  36.5 0.8 fusion.238
  37.3 3.3 %all-to-all-start.2 = ((f32[8,2,8]{2,1,0:T(2,128)}), f32[8,2,8]{2,1,0:T(2,128)S(1)}, u32[]{:S(2)}, u32[]{:S(2)}) async-start(f32[8,2,8]{2,1,0:T(2,128)} %bitcast.15), calls=%async_computation.2 | async-start | bytes 16384 | tf_op jit(solution)/shard_map/all_to_all | solution.py:76
  40.6 13.5 %all_gather.3 = f32[6,32,128]{2,1,0:T(8,128)S(1)} all-gather(f32[6,8,128]{2,1,0:T(8,128)S(1)} %copy-done.18), channel_id=1, replica_groups=mesh['domain'=8,'band'=4] {'band'}, dimensions={1}, use_global_device_ids=true | all-gather | bytes 122880 | tf_op jit(solution)/shard_map/all_gather | solution.py:54
  54.8 1.0 scatter_custom_fusion
  56.7 2.1 %broadcast_multiply_fusion = (f32[6,32,128]{2,1,0:T(8,128)S(1)}, f32[6,32,128]{2,1,0:T(8,128)S(1)}) fusion(f32[6,32,128]{2,1,0:T(8,128)S(1)} %bitcast.131, f32[6,32,128]{2,1,0:T(8,128)S(1)} %bitcast.135, f32[6,32,128]{2,1,0:T(8,128)S(1)} %all_gather.3, f32[6,32,6]{2,1,0:T(8,128)} %get-tuple-element.196, f32[6,32,122]{2,1,0:T(8,128)} %get-tuple-element.198, ...), kind=kLoop, calls=%fused_computation.315 | loop fusion | flops 2064384 | bytes 3047424 | tf_op jit(solution)/shard_map/div | solution.py:95
  61.3 1.9 %collective-permute-start.3 = (f32[6,32,128]{2,1,0:T(8,128)S(1)}, f32[6,32,128]{2,1,0:T(8,128)}, u32[]{:S(2)}, u32[]{:S(2)}) collective-permute-start(f32[6,32,128]{2,1,0:T(8,128)S(1)} %get-tuple-element.5), channel_id=1, source_target_pairs={{0,4},{4,8},{8,12},{12,16},{16,20},{20,24},{24,28},{1,5},{5,9},{9,... | collective-permute-start | bytes 294920 | tf_op jit(solution)/shard_map/ppermute | solution.py:28
  63.2 1.3 collective-permute-start.2
  69.6 0.8 gather_fusion.1
  70.4 1.1 fusion.10
  72.1 6.5 %all-to-all-start.3 = ((f32[8,2,8]{2,1,0:T(2,128)}), f32[8,2,8]{2,1,0:T(2,128)S(1)}, u32[]{:S(2)}, u32[]{:S(2)}) async-start(f32[8,2,8]{2,1,0:T(2,128)} %broadcast_multiply_fusion.3), calls=%async_computation.3 | async-start | bytes 16384 | tf_op jit(solution)/shard_map/all_to_all | solution.py:70
  79.2 4.1 %all-to-all-done.3 = f32[8,2,8]{2,1,0:T(2,128)S(1)} async-done(((f32[8,2,8]{2,1,0:T(2,128)}), f32[8,2,8]{2,1,0:T(2,128)S(1)}, u32[]{:S(2)}, u32[]{:S(2)}) %all-to-all-start.3) | async-done | bytes 544 | tf_op jit(solution)/shard_map/all_to_all | solution.py:70
  83.6 0.8 fusion.236
  84.4 3.3 %all-to-all-start.4 = ((f32[8,2,8]{2,1,0:T(2,128)}), f32[8,2,8]{2,1,0:T(2,128)S(1)}, u32[]{:S(2)}, u32[]{:S(2)}) async-start(f32[8,2,8]{2,1,0:T(2,128)} %bitcast.25), calls=%async_computation.4 | async-start | bytes 16384 | tf_op jit(solution)/shard_map/all_to_all | solution.py:76
  88.3 4.0 %all-to-all-done.4 = f32[8,2,8]{2,1,0:T(2,128)S(1)} async-done(((f32[8,2,8]{2,1,0:T(2,128)}), f32[8,2,8]{2,1,0:T(2,128)S(1)}, u32[]{:S(2)}, u32[]{:S(2)}) %all-to-all-start.4) | async-done | bytes 544 | tf_op jit(solution)/shard_map/all_to_all | solution.py:76
  93.0 1.2 scatter_custom_fusion.1
  95.0 2.1 %multiply_subtract_fusion.1 = f32[6,32,128]{2,1,0:T(8,128)S(1)} fusion(f32[6,32,128]{2,1,0:T(8,128)S(1)} %get-tuple-element.6, f32[6,32,128]{2,1,0:T(8,128)S(1)} %bitcast.136, f32[6,32,128]{2,1,0:T(8,128)S(1)} %all_gather.3, f32[6,32,128]{2,1,0:T(8,128)S(1)} %get-tuple-element.5, f32[6,32,6]{2,1,0:T(8,128)S(1)} %get-tuple-element.148, ...), kind=kLoop, calls=%fused_computation.310 | loop fusion | flops 2088960 | bytes 3145728 | tf_op jit(solution)/shard_map/sub | solution.py:98
  99.5 2.3 %collective-permute-start.5 = (f32[6,32,128]{2,1,0:T(8,128)S(1)}, f32[6,32,128]{2,1,0:T(8,128)}, u32[]{:S(2)}, u32[]{:S(2)}) collective-permute-start(f32[6,32,128]{2,1,0:T(8,128)S(1)} %multiply_subtract_fusion.1), channel_id=1, source_target_pairs={{0,4},{4,8},{8,12},{12,16},{16,20},{20,24},{24,28},{1,5},{5,9},{9,... | collective-permute-start | bytes 294920 | tf_op jit(solution)/shard_map/ppermute | solution.py:28
  101.9 1.3 collective-permute-start.4
  108.3 0.8 gather_fusion.2
  109.1 1.1 fusion.6
  110.8 4.7 %all-to-all-start.5 = ((f32[8,2,8]{2,1,0:T(2,128)}), f32[8,2,8]{2,1,0:T(2,128)S(1)}, u32[]{:S(2)}, u32[]{:S(2)}) async-start(f32[8,2,8]{2,1,0:T(2,128)} %broadcast_multiply_fusion.2), calls=%async_computation.5 | async-start | bytes 16384 | tf_op jit(solution)/shard_map/all_to_all | solution.py:70
  116.1 4.1 %all-to-all-done.5 = f32[8,2,8]{2,1,0:T(2,128)S(1)} async-done(((f32[8,2,8]{2,1,0:T(2,128)}), f32[8,2,8]{2,1,0:T(2,128)S(1)}, u32[]{:S(2)}, u32[]{:S(2)}) %all-to-all-start.5) | async-done | bytes 544 | tf_op jit(solution)/shard_map/all_to_all | solution.py:70
  120.4 0.8 fusion.234
  121.2 3.3 %all-to-all-start.6 = ((f32[8,2,8]{2,1,0:T(2,128)}), f32[8,2,8]{2,1,0:T(2,128)S(1)}, u32[]{:S(2)}, u32[]{:S(2)}) async-start(f32[8,2,8]{2,1,0:T(2,128)} %bitcast.35), calls=%async_computation.6 | async-start | bytes 16384 | tf_op jit(solution)/shard_map/all_to_all | solution.py:76
  125.2 4.0 %all-to-all-done.6 = f32[8,2,8]{2,1,0:T(2,128)S(1)} async-done(((f32[8,2,8]{2,1,0:T(2,128)}), f32[8,2,8]{2,1,0:T(2,128)S(1)}, u32[]{:S(2)}, u32[]{:S(2)}) %all-to-all-start.6) | async-done | bytes 544 | tf_op jit(solution)/shard_map/all_to_all | solution.py:76
  129.9 1.3 scatter_custom_fusion.2
  132.0 2.1 %multiply_subtract_fusion = f32[6,32,128]{2,1,0:T(8,128)S(1)} fusion(f32[6,32,128]{2,1,0:T(8,128)S(1)} %multiply_subtract_fusion.1, f32[6,32,128]{2,1,0:T(8,128)S(1)} %bitcast.137, f32[6,32,128]{2,1,0:T(8,128)S(1)} %all_gather.3, f32[6,32,6]{2,1,0:T(8,128)S(1)} %get-tuple-element.100, f32[6,32,122]{2,1,0:T(8,128)S(1)} %get-tuple-element.102, ...), kind=kLoop, calls=%fused_computation.309 | loop fusion | flops 2113536 | bytes 3047424 | tf_op jit(solution)/shard_map/sub | solution.py:98
  136.6 2.3 %collective-permute-start.7 = (f32[6,32,128]{2,1,0:T(8,128)S(1)}, f32[6,32,128]{2,1,0:T(8,128)}, u32[]{:S(2)}, u32[]{:S(2)}) collective-permute-start(f32[6,32,128]{2,1,0:T(8,128)S(1)} %multiply_subtract_fusion), channel_id=1, source_target_pairs={{0,4},{4,8},{8,12},{12,16},{16,20},{20,24},{24,28},{1,5},{5,9},{9,... | collective-permute-start | bytes 294920 | tf_op jit(solution)/shard_map/ppermute | solution.py:28
  138.9 1.3 collective-permute-start.6
  145.4 1.1 fusion.2
  147.2 4.7 %all-to-all-start.7 = ((f32[8,2,8]{2,1,0:T(2,128)}), f32[8,2,8]{2,1,0:T(2,128)S(1)}, u32[]{:S(2)}, u32[]{:S(2)}) async-start(f32[8,2,8]{2,1,0:T(2,128)} %broadcast_multiply_fusion.1), calls=%async_computation.7 | async-start | bytes 16384 | tf_op jit(solution)/shard_map/all_to_all | solution.py:70
  152.4 4.1 %all-to-all-done.7 = f32[8,2,8]{2,1,0:T(2,128)S(1)} async-done(((f32[8,2,8]{2,1,0:T(2,128)}), f32[8,2,8]{2,1,0:T(2,128)S(1)}, u32[]{:S(2)}, u32[]{:S(2)}) %all-to-all-start.7) | async-done | bytes 544 | tf_op jit(solution)/shard_map/all_to_all | solution.py:70
  156.8 0.8 fusion.232
  157.6 3.3 %all-to-all-start.8 = ((f32[8,2,8]{2,1,0:T(2,128)}), f32[8,2,8]{2,1,0:T(2,128)S(1)}, u32[]{:S(2)}, u32[]{:S(2)}) async-start(f32[8,2,8]{2,1,0:T(2,128)} %bitcast.45), calls=%async_computation.8 | async-start | bytes 16384 | tf_op jit(solution)/shard_map/all_to_all | solution.py:76
  160.9 4.6 %all-to-all-done.8 = f32[8,2,8]{2,1,0:T(2,128)S(1)} async-done(((f32[8,2,8]{2,1,0:T(2,128)}), f32[8,2,8]{2,1,0:T(2,128)S(1)}, u32[]{:S(2)}, u32[]{:S(2)}) %all-to-all-start.8) | async-done | bytes 544 | tf_op jit(solution)/shard_map/all_to_all | solution.py:76
  166.8 1.5 reshape.199
  168.3 1.3 scatter_custom_fusion.3
  170.4 2.7 %subtract_bitcast_fusion = f32[1,6,32,128]{3,2,1,0:T(8,128)} fusion(f32[6,32,128]{2,1,0:T(8,128)S(1)} %multiply_subtract_fusion.1, f32[6,32,128]{2,1,0:T(8,128)S(1)} %multiply_subtract_fusion, f32[6,32,128]{2,1,0:T(8,128)S(1)} %bitcast.134, f32[6,32,128]{2,1,0:T(8,128)S(1)} %all_gather.3, f32[6,32,6]{2,1,0:T(8,128)} %get-tuple-element.52, ...), kind=kLoop, calls=%fused_computation.308 | loop fusion | flops 2088960 | bytes 3047424 | tf_op jit(solution)/shard_map/broadcast_in_dim | solution.py:101
  (196 shorter events, 46.4 us)
Async XLA Ops:
  0.0 25.1 %copy-start = (f32[1,8,2,8,1024]{4,3,2,1,0:T(8,128)S(1)}, f32[1,8,2,8,1024]{4,3,2,1,0:T(8,128)}, u32[]{:S(2)}) copy-start(f32[1,8,2,8,1024]{4,3,2,1,0:T(8,128)} %param.8) | copy-start | bytes 1572868
  0.0 17.0 %copy-start.1 = (f32[1,6,32,128]{3,2,1,0:T(8,128)S(1)}, f32[1,6,32,128]{3,2,1,0:T(8,128)}, u32[]{:S(2)}) copy-start(f32[1,6,32,128]{3,2,1,0:T(8,128)} %param.6) | copy-start | bytes 294916
  0.0 55.9 %collective-permute-start.1 = (f32[6,32,128]{2,1,0:T(8,128)}, f32[6,32,128]{2,1,0:T(8,128)}, u32[]{:S(2)}, u32[]{:S(2)}) collective-permute-start(f32[6,32,128]{2,1,0:T(8,128)} %bitcast.104), channel_id=1, source_target_pairs={{0,4},{4,8},{8,12},{12,16},{16,20},{20,24},{24,28},{1,5},{5,9},{9,... | collective-permute-start | bytes 294920 | tf_op jit(solution)/shard_map/ppermute | solution.py:28
  3.1 52.8 %collective-permute-start = (f32[6,32,128]{2,1,0:T(8,128)}, f32[6,32,128]{2,1,0:T(8,128)}, u32[]{:S(2)}, u32[]{:S(2)}) collective-permute-start(f32[6,32,128]{2,1,0:T(8,128)} %bitcast.105), channel_id=1, source_target_pairs={{4,0},{8,4},{12,8},{16,12},{20,16},{24,20},{28,24},{5,1},{9,5},{13... | collective-permute-start | bytes 294920 | tf_op jit(solution)/shard_map/ppermute | solution.py:29
  5.8 21.1 %all-to-all-start = ((s32[8,1,2]{2,1,0:T(1,128)}), s32[8,1,2]{2,1,0:T(1,128)S(1)}, u32[]{:S(2)}, u32[]{:S(2)}) async-start(s32[8,1,2]{2,1,0:T(1,128)} %copy.22), calls=%async_computation | async-start | bytes 8192 | tf_op jit(solution)/shard_map/all_to_all | solution.py:64
  23.4 0.7 copy-start.23
  24.4 30.5 %copy-start.24 = (s32[128]{0:T(128)}, s32[128]{0:T(128)S(1)}, u32[]{:S(2)}) copy-start(s32[128]{0:T(128)S(1)} %fusion.249) | copy-start | bytes 1540
  24.4 0.7 copy-start.22
  26.8 8.9 %all-to-all-start.1 = ((f32[8,2,8]{2,1,0:T(2,128)}), f32[8,2,8]{2,1,0:T(2,128)S(1)}, u32[]{:S(2)}, u32[]{:S(2)}) async-start(f32[8,2,8]{2,1,0:T(2,128)} %broadcast_multiply_fusion.4), calls=%async_computation.1 | async-start | bytes 16384 | tf_op jit(solution)/shard_map/all_to_all | solution.py:70
  32.8 3.7 %copy-start.25 = (s32[16]{0:T(128)}, s32[16]{0:T(128)S(1)}, u32[]{:S(2)}) copy-start(s32[16]{0:T(128)S(1)} %eq.15) | copy-start | bytes 196
  35.7 0.8 copy-start.2
  36.5 4.1 %copy-start.18 = (f32[6,8,128]{2,1,0:T(8,128)S(1)}, f32[6,8,128]{2,1,0:T(8,128)}, u32[]{:S(2)}) copy-start(f32[6,8,128]{2,1,0:T(8,128)} %param.7) | copy-start | bytes 73732
  37.3 16.8 %all-to-all-start.2 = ((f32[8,2,8]{2,1,0:T(2,128)}), f32[8,2,8]{2,1,0:T(2,128)S(1)}, u32[]{:S(2)}, u32[]{:S(2)}) async-start(f32[8,2,8]{2,1,0:T(2,128)} %bitcast.15), calls=%async_computation.2 | async-start | bytes 16384 | tf_op jit(solution)/shard_map/all_to_all | solution.py:76
  55.9 0.7 copy-start.20
  55.9 0.7 copy-start.21
  55.9 0.7 copy-start.5
  55.9 0.7 copy-start.4
  55.9 0.8 copy-start.3
  61.3 32.9 %collective-permute-start.3 = (f32[6,32,128]{2,1,0:T(8,128)S(1)}, f32[6,32,128]{2,1,0:T(8,128)}, u32[]{:S(2)}, u32[]{:S(2)}) collective-permute-start(f32[6,32,128]{2,1,0:T(8,128)S(1)} %get-tuple-element.5), channel_id=1, source_target_pairs={{0,4},{4,8},{8,12},{12,16},{16,20},{20,24},{24,28},{1,5},{5,9},{9,... | collective-permute-start | bytes 294920 | tf_op jit(solution)/shard_map/ppermute | solution.py:28
  63.2 31.0 %collective-permute-start.2 = (f32[6,32,128]{2,1,0:T(8,128)S(1)}, f32[6,32,128]{2,1,0:T(8,128)}, u32[]{:S(2)}, u32[]{:S(2)}) collective-permute-start(f32[6,32,128]{2,1,0:T(8,128)S(1)} %get-tuple-element.5), channel_id=1, source_target_pairs={{4,0},{8,4},{12,8},{16,12},{20,16},{24,20},{28,24},{5,1},{9,5},{13... | collective-permute-start | bytes 294920 | tf_op jit(solution)/shard_map/ppermute | solution.py:29
  72.1 11.2 %all-to-all-start.3 = ((f32[8,2,8]{2,1,0:T(2,128)}), f32[8,2,8]{2,1,0:T(2,128)S(1)}, u32[]{:S(2)}, u32[]{:S(2)}) async-start(f32[8,2,8]{2,1,0:T(2,128)} %broadcast_multiply_fusion.3), calls=%async_computation.3 | async-start | bytes 16384 | tf_op jit(solution)/shard_map/all_to_all | solution.py:70
  79.2 4.1 %copy-start.26 = (s32[16]{0:T(128)S(1)}, s32[16]{0:T(128)}, u32[]{:S(2)}) copy-start(s32[16]{0:T(128)} %copy-done.25) | copy-start | bytes 196
  84.4 8.0 %all-to-all-start.4 = ((f32[8,2,8]{2,1,0:T(2,128)}), f32[8,2,8]{2,1,0:T(2,128)S(1)}, u32[]{:S(2)}, u32[]{:S(2)}) async-start(f32[8,2,8]{2,1,0:T(2,128)} %bitcast.25), calls=%async_computation.4 | async-start | bytes 16384 | tf_op jit(solution)/shard_map/all_to_all | solution.py:76
  94.2 0.7 copy-start.16
  94.2 0.7 copy-start.11
  94.2 0.8 copy-start.10
  94.2 0.8 copy-start.9
  99.5 31.7 %collective-permute-start.5 = (f32[6,32,128]{2,1,0:T(8,128)S(1)}, f32[6,32,128]{2,1,0:T(8,128)}, u32[]{:S(2)}, u32[]{:S(2)}) collective-permute-start(f32[6,32,128]{2,1,0:T(8,128)S(1)} %multiply_subtract_fusion.1), channel_id=1, source_target_pairs={{0,4},{4,8},{8,12},{12,16},{16,20},{20,24},{24,28},{1,5},{5,9},{9,... | collective-permute-start | bytes 294920 | tf_op jit(solution)/shard_map/ppermute | solution.py:28
  101.9 29.4 %collective-permute-start.4 = (f32[6,32,128]{2,1,0:T(8,128)S(1)}, f32[6,32,128]{2,1,0:T(8,128)}, u32[]{:S(2)}, u32[]{:S(2)}) collective-permute-start(f32[6,32,128]{2,1,0:T(8,128)S(1)} %multiply_subtract_fusion.1), channel_id=1, source_target_pairs={{4,0},{8,4},{12,8},{16,12},{20,16},{24,20},{28,24},{5,1},{9,5},{13... | collective-permute-start | bytes 294920 | tf_op jit(solution)/shard_map/ppermute | solution.py:29
  110.8 9.4 %all-to-all-start.5 = ((f32[8,2,8]{2,1,0:T(2,128)}), f32[8,2,8]{2,1,0:T(2,128)S(1)}, u32[]{:S(2)}, u32[]{:S(2)}) async-start(f32[8,2,8]{2,1,0:T(2,128)} %broadcast_multiply_fusion.2), calls=%async_computation.5 | async-start | bytes 16384 | tf_op jit(solution)/shard_map/all_to_all | solution.py:70
  116.1 4.1 %copy-start.27 = (s32[16]{0:T(128)S(1)}, s32[16]{0:T(128)}, u32[]{:S(2)}) copy-start(s32[16]{0:T(128)} %copy-done.25) | copy-start | bytes 196
  121.2 8.0 %all-to-all-start.6 = ((f32[8,2,8]{2,1,0:T(2,128)}), f32[8,2,8]{2,1,0:T(2,128)S(1)}, u32[]{:S(2)}, u32[]{:S(2)}) async-start(f32[8,2,8]{2,1,0:T(2,128)} %bitcast.35), calls=%async_computation.6 | async-start | bytes 16384 | tf_op jit(solution)/shard_map/all_to_all | solution.py:76
  131.2 0.7 copy-start.17
  131.2 0.7 copy-start.14
  131.3 0.8 copy-start.13
  131.3 0.8 copy-start.12
  136.6 33.1 %collective-permute-start.7 = (f32[6,32,128]{2,1,0:T(8,128)S(1)}, f32[6,32,128]{2,1,0:T(8,128)}, u32[]{:S(2)}, u32[]{:S(2)}) collective-permute-start(f32[6,32,128]{2,1,0:T(8,128)S(1)} %multiply_subtract_fusion), channel_id=1, source_target_pairs={{0,4},{4,8},{8,12},{12,16},{16,20},{20,24},{24,28},{1,5},{5,9},{9,... | collective-permute-start | bytes 294920 | tf_op jit(solution)/shard_map/ppermute | solution.py:28
  138.9 30.8 %collective-permute-start.6 = (f32[6,32,128]{2,1,0:T(8,128)S(1)}, f32[6,32,128]{2,1,0:T(8,128)}, u32[]{:S(2)}, u32[]{:S(2)}) collective-permute-start(f32[6,32,128]{2,1,0:T(8,128)S(1)} %multiply_subtract_fusion), channel_id=1, source_target_pairs={{4,0},{8,4},{12,8},{16,12},{20,16},{24,20},{28,24},{5,1},{9,5},{13... | collective-permute-start | bytes 294920 | tf_op jit(solution)/shard_map/ppermute | solution.py:29
  147.2 9.4 %all-to-all-start.7 = ((f32[8,2,8]{2,1,0:T(2,128)}), f32[8,2,8]{2,1,0:T(2,128)S(1)}, u32[]{:S(2)}, u32[]{:S(2)}) async-start(f32[8,2,8]{2,1,0:T(2,128)} %broadcast_multiply_fusion.1), calls=%async_computation.7 | async-start | bytes 16384 | tf_op jit(solution)/shard_map/all_to_all | solution.py:70
  152.4 4.1 %copy-start.28 = (s32[16]{0:T(128)S(1)}, s32[16]{0:T(128)}, u32[]{:S(2)}) copy-start(s32[16]{0:T(128)} %copy-done.25) | copy-start | bytes 196
  157.6 8.0 %all-to-all-start.8 = ((f32[8,2,8]{2,1,0:T(2,128)}), f32[8,2,8]{2,1,0:T(2,128)S(1)}, u32[]{:S(2)}, u32[]{:S(2)}) async-start(f32[8,2,8]{2,1,0:T(2,128)} %bitcast.45), calls=%async_computation.8 | async-start | bytes 16384 | tf_op jit(solution)/shard_map/all_to_all | solution.py:76
  168.3 1.4 copy-start.19
  169.7 0.7 copy-start.15
  169.7 0.7 copy-start.8
  169.7 0.8 copy-start.7
  169.7 0.8 copy-start.6
where the time goes:
time: 175 us; the launch traced here: 173 us
  starting transfers between devices  54.7 us (31%)
  local copies, waits for them, and re-layouts  47.6 us (27%)
  waiting for transfers between devices  27.9 us (16%)
  other arithmetic  18.2 us (10%)
  blocking collectives  13.5 us (8%)
  matrix products  10.3 us (6%)
    slice x48, local copies, waits for them, and re-layouts, kinetic(): jnp.roll(grid_field, distance, 1)  21.3 us
    all_to_all x4, starting transfers between devices, owner_side(): lax.all_to_all(partial_value, 'domain', split_axis=0, concat_axis=0, tile...  20.1 us
    all_to_all x4, waiting for transfers between devices, owner_side(): lax.all_to_all(partial_value, 'domain', split_axis=0, concat_axis=0, tile...  15.2 us
    slice x48, local copies, waits for them, and re-layouts, kinetic(): jnp.roll(grid_field, distance, 2)  14.5 us
    all_gather x1, blocking collectives, shards(): pot_full = lax.all_gather(potential, 'band', axis=1, tiled=True)  13.5 us
    all_to_all x4, starting transfers between devices, owner_side(): lax.all_to_all(returned, 'domain', split_axis=0, concat_axis=0, tiled=True)  13.3 us
    all_to_all x4, waiting for transfers between devices, owner_side(): lax.all_to_all(returned, 'domain', split_axis=0, concat_axis=0, tiled=True)  12.7 us
    ppermute x4, starting transfers between devices, extended(): before = lax.ppermute(last, axis, up)  9.69 us
  transfers between devices with their start and end apart: 17, of which 7 were waited for; matrix products, arithmetic and copies ran while one was open for 32% of the time, Pallas kernels for 0%

commit v1 on v0

--- a/solution.py
+++ b/solution.py
@@ -16,6 +16,22 @@
 filter_center = 6.0
 filter_half_width = 4.0
 highest = lax.Precision.HIGHEST
+
+
+def swapped_with_each(x, axis, split, join):
+    ways, here = (lax.axis_size(axis), lax.axis_index(axis))
+    width = x.shape[split] // ways
+    lengths = list(x.shape)
+    lengths[split] = width
+    height = lengths[join]
+    lengths[join] = height * ways
+    full = jnp.zeros(lengths, x.dtype)
+    for mask in range(ways):
+        part = lax.dynamic_slice_in_dim(x, (here ^ mask) * width, width, axis=split)
+        if mask:
+            part = lax.ppermute(part, axis, [(d, d ^ mask) for d in range(ways)])
+        full = lax.dynamic_update_slice_in_dim(full, part, (here ^ mask) * height, axis=join)
+    return full
 
 
 def extended(value, sides, width):
@@ -61,7 +77,7 @@
     slot_atoms = intersection[0]
     live_slots = (slot_atoms >= 0).astype(jnp.float32)
     atom_count = dmat.shape[0]
-    incoming = lax.all_to_all(slot_atoms, "domain", split_axis=0, concat_axis=0, tiled=True)
+    incoming = swapped_with_each(slot_atoms, "domain", 0, 0)
     in_hot = (incoming.reshape(-1)[:, None] == jnp.arange(atom_count, dtype=jnp.int32)).astype(
         jnp.float32
     )

time: 175 us -> 184 us (1.051)
  starting transfers between devices: 54.7 us -> 59.7 us
  waiting for transfers between devices: 27.9 us -> 32.4 us
  local copies, waits for them, and re-layouts: 47.6 us -> 45.6 us
    ppermute x0 -> x7, starting transfers between devices: none -> 11.1 us  [swapped_with_each(): part = lax.ppermute(part, axis, [(d, d ^ mask) for d in range(ways)])]
    ppermute x0 -> x7, waiting for transfers between devices: none -> 8 us  [swapped_with_each(): part = lax.ppermute(part, axis, [(d, d ^ mask) for d in range(ways)])]
    all_to_all x1 -> x0, starting transfers between devices: 6.47 us -> none  [shards(): lax.all_to_all(slot_atoms, 'domain', split_axis=0, concat_axis=0, tiled=T...]
    all_to_all x4, waiting for transfers between devices: 15.2 us -> 12.3 us  [owner_side(): lax.all_to_all(partial_value, 'domain', split_axis=0, concat_axis=0, tile...]
    all_to_all x2 -> x0, local copies, waits for them, and re-layouts: 1.84 us -> none  [shards(): lax.all_to_all(slot_atoms, 'domain', split_axis=0, concat_axis=0, tiled=T...]
    unnamed x58 -> x65, local copies, waits for them, and re-layouts: 4.31 us -> 3.92 us
  transfers between devices with their start and end apart: 17 -> 23, of which waited for: 7 -> 10; matrix products, arithmetic and copies ran while one was open for 32% -> 30% of each run, Pallas kernels for 0% -> 0%
where the time goes in v1:
time: 184 us; the launch traced here: 182 us
  starting transfers between devices  59.7 us (32%)
  local copies, waits for them, and re-layouts  45.6 us (25%)
  waiting for transfers between devices  32.4 us (18%)
  other arithmetic  17.7 us (10%)
  blocking collectives  13.5 us (7%)
  matrix products  12.1 us (7%)
    slice x48, local copies, waits for them, and re-layouts, kinetic(): jnp.roll(grid_field, distance, 1)  20.9 us
    all_to_all x4, starting transfers between devices, owner_side(): lax.all_to_all(partial_value, 'domain', split_axis=0, concat_axis=0, tile...  20.1 us
    slice x48, local copies, waits for them, and re-layouts, kinetic(): jnp.roll(grid_field, distance, 2)  14.4 us
    all_to_all x4, starting transfers between devices, owner_side(): lax.all_to_all(returned, 'domain', split_axis=0, concat_axis=0, tiled=True)  14.3 us
    all_gather x1, blocking collectives, shards(): pot_full = lax.all_gather(potential, 'band', axis=1, tiled=True)  13.5 us
    all_to_all x4, waiting for transfers between devices, owner_side(): lax.all_to_all(partial_value, 'domain', split_axis=0, concat_axis=0, tile...  12.3 us
    all_to_all x4, waiting for transfers between devices, owner_side(): lax.all_to_all(returned, 'domain', split_axis=0, concat_axis=0, tiled=True)  12.1 us
    ppermute x7, starting transfers between devices, swapped_with_each(): part = lax.ppermute(part, axis, [(d, d ^ mask) for d in range(ways)])  11.1 us
  transfers between devices with their start and end apart: 23, of which 10 were waited for; matrix products, arithmetic and copies ran while one was open for 30% of the time, Pallas kernels for 0%

profile of v1, /device:TPU:0, one launch (start us, length us, event | category | flops | bytes accessed | tf_op | source)
XLA Modules:
  0.0 182.1 jit_solution(5039480277541216095)
XLA Ops:
  0.0 2.5 %collective-permute-start.1 = (f32[6,32,128]{2,1,0:T(8,128)}, f32[6,32,128]{2,1,0:T(8,128)S(1)}, u32[]{:S(2)}, u32[]{:S(2)}) collective-permute-start(f32[6,32,128]{2,1,0:T(8,128)} %bitcast.131), channel_id=1, source_target_pairs={{0,4},{4,8},{8,12},{12,16},{16,20},{20,24},{24,28},{1,5},{5,9},{9,... | collective-permute-start | bytes 294920 | tf_op jit(solution)/shard_map/ppermute | solution.py:44
  2.5 1.3 collective-permute-start
  3.8 1.3 fusion.256
  5.1 5.9 %collective-permute-start.7 = (s32[1,2]{1,0:T(1,128)S(1)}, s32[1,2]{1,0:T(1,128)S(1)}, u32[]{:S(2)}, u32[]{:S(2)}) collective-permute-start(s32[1,2]{1,0:T(1,128)S(1)} %bitcast.196), channel_id=1, source_target_pairs={{0,24},{4,28},{8,16},{12,20},{16,8},{20,12},{24,0},{28,4},{1,25},{... | collective-permute-start | bytes 32 | tf_op jit(solution)/shard_map/ppermute | solution.py:32
  13.6 1.1 fusion.14
  15.3 4.1 %all-to-all-start = ((f32[8,2,8]{2,1,0:T(2,128)}), f32[8,2,8]{2,1,0:T(2,128)S(1)}, u32[]{:S(2)}, u32[]{:S(2)}) async-start(f32[8,2,8]{2,1,0:T(2,128)} %broadcast_multiply_fusion.4), calls=%async_computation | async-start | bytes 16384 | tf_op jit(solution)/shard_map/all_to_all | solution.py:86
  28.5 2.1 %collective-permute-start.3 = (s32[1,2]{1,0:T(1,128)S(1)}, s32[1,2]{1,0:T(1,128)S(1)}, u32[]{:S(2)}, u32[]{:S(2)}) collective-permute-start(s32[1,2]{1,0:T(1,128)S(1)} %bitcast.200), channel_id=1, source_target_pairs={{0,8},{4,12},{8,0},{12,4},{16,24},{20,28},{24,16},{28,20},{1,9},{5... | collective-permute-start | bytes 32 | tf_op jit(solution)/shard_map/ppermute | solution.py:32
  30.6 1.5 collective-permute-done.3
  32.7 2.3 %collective-permute-done.4 = s32[1,2]{1,0:T(1,128)S(1)} collective-permute-done((s32[1,2]{1,0:T(1,128)S(1)}, s32[1,2]{1,0:T(1,128)S(1)}, u32[]{:S(2)}, u32[]{:S(2)}) %collective-permute-start.4) | collective-permute-done | bytes 40 | tf_op jit(solution)/shard_map/ppermute | solution.py:32
  35.0 2.0 %collective-permute-start.5 = (s32[1,2]{1,0:T(1,128)S(1)}, s32[1,2]{1,0:T(1,128)S(1)}, u32[]{:S(2)}, u32[]{:S(2)}) collective-permute-start(s32[1,2]{1,0:T(1,128)S(1)} %bitcast.198), channel_id=1, source_target_pairs={{0,16},{4,20},{8,24},{12,28},{16,0},{20,4},{24,8},{28,12},{1,17},{... | collective-permute-start | bytes 32 | tf_op jit(solution)/shard_map/ppermute | solution.py:32
  37.1 1.5 collective-permute-done.5
  38.9 2.7 %collective-permute-done.6 = s32[1,2]{1,0:T(1,128)S(1)} collective-permute-done((s32[1,2]{1,0:T(1,128)S(1)}, s32[1,2]{1,0:T(1,128)S(1)}, u32[]{:S(2)}, u32[]{:S(2)}) %collective-permute-start.6) | collective-permute-done | bytes 40 | tf_op jit(solution)/shard_map/ppermute | solution.py:32
  42.4 0.8 fusion.238
  43.2 4.2 %all-to-all-start.1 = ((f32[8,2,8]{2,1,0:T(2,128)}), f32[8,2,8]{2,1,0:T(2,128)S(1)}, u32[]{:S(2)}, u32[]{:S(2)}) async-start(f32[8,2,8]{2,1,0:T(2,128)} %bitcast.14), calls=%async_computation.1 | async-start | bytes 16384 | tf_op jit(solution)/shard_map/all_to_all | solution.py:92
  47.4 13.5 %all_gather.3 = f32[6,32,128]{2,1,0:T(8,128)S(1)} all-gather(f32[6,8,128]{2,1,0:T(8,128)S(1)} %copy-done.20), channel_id=1, replica_groups=mesh['domain'=8,'band'=4] {'band'}, dimensions={1}, use_global_device_ids=true | all-gather | bytes 122880 | tf_op jit(solution)/shard_map/all_gather | solution.py:70
  62.1 1.3 scatter_custom_fusion
  64.3 2.1 %broadcast_multiply_fusion = (f32[6,32,128]{2,1,0:T(8,128)S(1)}, f32[6,32,128]{2,1,0:T(8,128)S(1)}) fusion(f32[6,32,128]{2,1,0:T(8,128)S(1)} %bitcast.158, f32[6,32,128]{2,1,0:T(8,128)S(1)} %bitcast.162, f32[6,32,128]{2,1,0:T(8,128)S(1)} %all_gather.3, f32[6,32,6]{2,1,0:T(8,128)} %get-tuple-element.204, f32[6,32,122]{2,1,0:T(8,128)} %get-tuple-element.206, ...), kind=kLoop, calls=%fused_computation.315 | loop fusion | flops 2064384 | bytes 3047424 | tf_op jit(solution)/shard_map/div | solution.py:111
  68.9 1.9 %collective-permute-start.10 = (f32[6,32,128]{2,1,0:T(8,128)S(1)}, f32[6,32,128]{2,1,0:T(8,128)}, u32[]{:S(2)}, u32[]{:S(2)}) collective-permute-start(f32[6,32,128]{2,1,0:T(8,128)S(1)} %get-tuple-element.13), channel_id=1, source_target_pairs={{0,4},{4,8},{8,12},{12,16},{16,20},{20,24},{24,28},{1,5},{5,9},{9,... | collective-permute-start | bytes 294920 | tf_op jit(solution)/shard_map/ppermute | solution.py:44
  70.8 1.3 collective-permute-start.9
  77.8 0.8 gather_fusion.1
  78.6 1.1 fusion.10
  80.3 6.6 %all-to-all-start.2 = ((f32[8,2,8]{2,1,0:T(2,128)}), f32[8,2,8]{2,1,0:T(2,128)S(1)}, u32[]{:S(2)}, u32[]{:S(2)}) async-start(f32[8,2,8]{2,1,0:T(2,128)} %broadcast_multiply_fusion.3), calls=%async_computation.2 | async-start | bytes 16384 | tf_op jit(solution)/shard_map/all_to_all | solution.py:86
  87.6 4.1 %all-to-all-done.2 = f32[8,2,8]{2,1,0:T(2,128)S(1)} async-done(((f32[8,2,8]{2,1,0:T(2,128)}), f32[8,2,8]{2,1,0:T(2,128)S(1)}, u32[]{:S(2)}, u32[]{:S(2)}) %all-to-all-start.2) | async-done | bytes 544 | tf_op jit(solution)/shard_map/all_to_all | solution.py:86
  92.3 0.8 fusion.236
  93.1 3.3 %all-to-all-start.3 = ((f32[8,2,8]{2,1,0:T(2,128)}), f32[8,2,8]{2,1,0:T(2,128)S(1)}, u32[]{:S(2)}, u32[]{:S(2)}) async-start(f32[8,2,8]{2,1,0:T(2,128)} %bitcast.28), calls=%async_computation.3 | async-start | bytes 16384 | tf_op jit(solution)/shard_map/all_to_all | solution.py:92
  97.1 4.0 %all-to-all-done.3 = f32[8,2,8]{2,1,0:T(2,128)S(1)} async-done(((f32[8,2,8]{2,1,0:T(2,128)}), f32[8,2,8]{2,1,0:T(2,128)S(1)}, u32[]{:S(2)}, u32[]{:S(2)}) %all-to-all-start.3) | async-done | bytes 544 | tf_op jit(solution)/shard_map/all_to_all | solution.py:92
  101.8 1.2 scatter_custom_fusion.1
  103.8 2.2 %multiply_subtract_fusion.1 = f32[6,32,128]{2,1,0:T(8,128)S(1)} fusion(f32[6,32,128]{2,1,0:T(8,128)S(1)} %get-tuple-element.14, f32[6,32,128]{2,1,0:T(8,128)S(1)} %bitcast.163, f32[6,32,128]{2,1,0:T(8,128)S(1)} %all_gather.3, f32[6,32,128]{2,1,0:T(8,128)S(1)} %get-tuple-element.13, f32[6,32,6]{2,1,0:T(8,128)S(1)} %get-tuple-element.156, ...), kind=kLoop, calls=%fused_computation.310 | loop fusion | flops 2088960 | bytes 3145728 | tf_op jit(solution)/shard_map/sub | solution.py:114
  108.4 2.3 %collective-permute-start.12 = (f32[6,32,128]{2,1,0:T(8,128)S(1)}, f32[6,32,128]{2,1,0:T(8,128)}, u32[]{:S(2)}, u32[]{:S(2)}) collective-permute-start(f32[6,32,128]{2,1,0:T(8,128)S(1)} %multiply_subtract_fusion.1), channel_id=1, source_target_pairs={{0,4},{4,8},{8,12},{12,16},{16,20},{20,24},{24,28},{1,5},{5,9},{9,... | collective-permute-start | bytes 294920 | tf_op jit(solution)/shard_map/ppermute | solution.py:44
  110.7 1.3 collective-permute-start.11
  117.9 1.1 fusion.6
  119.7 4.7 %all-to-all-start.4 = ((f32[8,2,8]{2,1,0:T(2,128)}), f32[8,2,8]{2,1,0:T(2,128)S(1)}, u32[]{:S(2)}, u32[]{:S(2)}) async-start(f32[8,2,8]{2,1,0:T(2,128)} %broadcast_multiply_fusion.2), calls=%async_computation.4 | async-start | bytes 16384 | tf_op jit(solution)/shard_map/all_to_all | solution.py:86
  124.9 4.1 %all-to-all-done.4 = f32[8,2,8]{2,1,0:T(2,128)S(1)} async-done(((f32[8,2,8]{2,1,0:T(2,128)}), f32[8,2,8]{2,1,0:T(2,128)S(1)}, u32[]{:S(2)}, u32[]{:S(2)}) %all-to-all-start.4) | async-done | bytes 544 | tf_op jit(solution)/shard_map/all_to_all | solution.py:86
  129.7 0.8 fusion.234
  130.5 3.5 %all-to-all-start.5 = ((f32[8,2,8]{2,1,0:T(2,128)}), f32[8,2,8]{2,1,0:T(2,128)S(1)}, u32[]{:S(2)}, u32[]{:S(2)}) async-start(f32[8,2,8]{2,1,0:T(2,128)} %bitcast.42), calls=%async_computation.5 | async-start | bytes 16384 | tf_op jit(solution)/shard_map/all_to_all | solution.py:92
  134.6 4.0 %all-to-all-done.5 = f32[8,2,8]{2,1,0:T(2,128)S(1)} async-done(((f32[8,2,8]{2,1,0:T(2,128)}), f32[8,2,8]{2,1,0:T(2,128)S(1)}, u32[]{:S(2)}, u32[]{:S(2)}) %all-to-all-start.5) | async-done | bytes 544 | tf_op jit(solution)/shard_map/all_to_all | solution.py:92
  139.3 1.2 scatter_custom_fusion.2
  141.3 2.2 %multiply_subtract_fusion = f32[6,32,128]{2,1,0:T(8,128)S(1)} fusion(f32[6,32,128]{2,1,0:T(8,128)S(1)} %multiply_subtract_fusion.1, f32[6,32,128]{2,1,0:T(8,128)S(1)} %bitcast.164, f32[6,32,128]{2,1,0:T(8,128)S(1)} %all_gather.3, f32[6,32,6]{2,1,0:T(8,128)S(1)} %get-tuple-element.108, f32[6,32,122]{2,1,0:T(8,128)S(1)} %get-tuple-element.110, ...), kind=kLoop, calls=%fused_computation.309 | loop fusion | flops 2113536 | bytes 3047424 | tf_op jit(solution)/shard_map/sub | solution.py:114
  145.9 2.3 %collective-permute-start.14 = (f32[6,32,128]{2,1,0:T(8,128)S(1)}, f32[6,32,128]{2,1,0:T(8,128)}, u32[]{:S(2)}, u32[]{:S(2)}) collective-permute-start(f32[6,32,128]{2,1,0:T(8,128)S(1)} %multiply_subtract_fusion), channel_id=1, source_target_pairs={{0,4},{4,8},{8,12},{12,16},{16,20},{20,24},{24,28},{1,5},{5,9},{9,... | collective-permute-start | bytes 294920 | tf_op jit(solution)/shard_map/ppermute | solution.py:44
  148.2 1.3 collective-permute-start.13
  155.4 1.1 fusion.2
  157.1 4.7 %all-to-all-start.6 = ((f32[8,2,8]{2,1,0:T(2,128)}), f32[8,2,8]{2,1,0:T(2,128)S(1)}, u32[]{:S(2)}, u32[]{:S(2)}) async-start(f32[8,2,8]{2,1,0:T(2,128)} %broadcast_multiply_fusion.1), calls=%async_computation.6 | async-start | bytes 16384 | tf_op jit(solution)/shard_map/all_to_all | solution.py:86
  162.4 4.1 %all-to-all-done.6 = f32[8,2,8]{2,1,0:T(2,128)S(1)} async-done(((f32[8,2,8]{2,1,0:T(2,128)}), f32[8,2,8]{2,1,0:T(2,128)S(1)}, u32[]{:S(2)}, u32[]{:S(2)}) %all-to-all-start.6) | async-done | bytes 544 | tf_op jit(solution)/shard_map/all_to_all | solution.py:86
  167.1 0.8 fusion.232
  167.9 3.3 %all-to-all-start.7 = ((f32[8,2,8]{2,1,0:T(2,128)}), f32[8,2,8]{2,1,0:T(2,128)S(1)}, u32[]{:S(2)}, u32[]{:S(2)}) async-start(f32[8,2,8]{2,1,0:T(2,128)} %bitcast.56), calls=%async_computation.7 | async-start | bytes 16384 | tf_op jit(solution)/shard_map/all_to_all | solution.py:92
  171.8 4.0 %all-to-all-done.7 = f32[8,2,8]{2,1,0:T(2,128)S(1)} async-done(((f32[8,2,8]{2,1,0:T(2,128)}), f32[8,2,8]{2,1,0:T(2,128)S(1)}, u32[]{:S(2)}, u32[]{:S(2)}) %all-to-all-start.7) | async-done | bytes 544 | tf_op jit(solution)/shard_map/all_to_all | solution.py:92
  177.2 1.4 scatter_custom_fusion.3
  179.4 2.7 %subtract_bitcast_fusion = f32[1,6,32,128]{3,2,1,0:T(8,128)} fusion(f32[6,32,128]{2,1,0:T(8,128)S(1)} %multiply_subtract_fusion.1, f32[6,32,128]{2,1,0:T(8,128)S(1)} %multiply_subtract_fusion, f32[6,32,128]{2,1,0:T(8,128)S(1)} %bitcast.161, f32[6,32,128]{2,1,0:T(8,128)S(1)} %all_gather.3, f32[6,32,6]{2,1,0:T(8,128)} %get-tuple-element.60, ...), kind=kLoop, calls=%fused_computation.308 | loop fusion | flops 2088960 | bytes 3047424 | tf_op jit(solution)/shard_map/broadcast_in_dim | solution.py:117
  (222 shorter events, 52.9 us)
Async XLA Ops:
  0.0 13.6 %copy-start = (f32[1,8,2,8,1024]{4,3,2,1,0:T(8,128)S(1)}, f32[1,8,2,8,1024]{4,3,2,1,0:T(8,128)}, u32[]{:S(2)}) copy-start(f32[1,8,2,8,1024]{4,3,2,1,0:T(8,128)} %param.8) | copy-start | bytes 1572868
  0.0 12.9 %copy-start.1 = (f32[1,6,32,128]{3,2,1,0:T(8,128)S(1)}, f32[1,6,32,128]{3,2,1,0:T(8,128)}, u32[]{:S(2)}) copy-start(f32[1,6,32,128]{3,2,1,0:T(8,128)} %param.6) | copy-start | bytes 294916
  0.0 63.5 %collective-permute-start.1 = (f32[6,32,128]{2,1,0:T(8,128)}, f32[6,32,128]{2,1,0:T(8,128)S(1)}, u32[]{:S(2)}, u32[]{:S(2)}) collective-permute-start(f32[6,32,128]{2,1,0:T(8,128)} %bitcast.131), channel_id=1, source_target_pairs={{0,4},{4,8},{8,12},{12,16},{16,20},{20,24},{24,28},{1,5},{5,9},{9,... | collective-permute-start | bytes 294920 | tf_op jit(solution)/shard_map/ppermute | solution.py:44
  2.5 61.0 %collective-permute-start = (f32[6,32,128]{2,1,0:T(8,128)}, f32[6,32,128]{2,1,0:T(8,128)}, u32[]{:S(2)}, u32[]{:S(2)}) collective-permute-start(f32[6,32,128]{2,1,0:T(8,128)} %bitcast.132), channel_id=1, source_target_pairs={{4,0},{8,4},{12,8},{16,12},{20,16},{24,20},{28,24},{5,1},{9,5},{13... | collective-permute-start | bytes 294920 | tf_op jit(solution)/shard_map/ppermute | solution.py:45
  5.1 36.5 %collective-permute-start.7 = (s32[1,2]{1,0:T(1,128)S(1)}, s32[1,2]{1,0:T(1,128)S(1)}, u32[]{:S(2)}, u32[]{:S(2)}) collective-permute-start(s32[1,2]{1,0:T(1,128)S(1)} %bitcast.196), channel_id=1, source_target_pairs={{0,24},{4,28},{8,16},{12,20},{16,8},{20,12},{24,0},{28,4},{1,25},{... | collective-permute-start | bytes 32 | tf_op jit(solution)/shard_map/ppermute | solution.py:32
  11.0 30.6 %collective-permute-start.8 = (s32[1,2]{1,0:T(1,128)S(1)}, s32[1,2]{1,0:T(1,128)S(1)}, u32[]{:S(2)}, u32[]{:S(2)}) collective-permute-start(s32[1,2]{1,0:T(1,128)S(1)} %bitcast.195), channel_id=1, source_target_pairs={{0,28},{4,24},{8,20},{12,16},{16,12},{20,8},{24,4},{28,0},{1,29},{... | collective-permute-start | bytes 32 | tf_op jit(solution)/shard_map/ppermute | solution.py:32
  11.0 17.5 %collective-permute-start.2 = (s32[1,2]{1,0:T(1,128)S(1)}, s32[1,2]{1,0:T(1,128)S(1)}, u32[]{:S(2)}, u32[]{:S(2)}) collective-permute-start(s32[1,2]{1,0:T(1,128)S(1)} %bitcast.201), channel_id=1, source_target_pairs={{0,4},{4,0},{8,12},{12,8},{16,20},{20,16},{24,28},{28,24},{1,5},{5... | collective-permute-start | bytes 32 | tf_op jit(solution)/shard_map/ppermute | solution.py:32
  12.9 49.2 %copy-start.27 = (s32[128]{0:T(128)}, s32[128]{0:T(128)S(1)}, u32[]{:S(2)}) copy-start(s32[128]{0:T(128)S(1)} %fusion.257) | copy-start | bytes 1540
  15.3 26.4 %all-to-all-start = ((f32[8,2,8]{2,1,0:T(2,128)}), f32[8,2,8]{2,1,0:T(2,128)S(1)}, u32[]{:S(2)}, u32[]{:S(2)}) async-start(f32[8,2,8]{2,1,0:T(2,128)} %broadcast_multiply_fusion.4), calls=%async_computation | async-start | bytes 16384 | tf_op jit(solution)/shard_map/all_to_all | solution.py:86
  27.5 0.8 copy-start.19
  28.5 3.6 %collective-permute-start.3 = (s32[1,2]{1,0:T(1,128)S(1)}, s32[1,2]{1,0:T(1,128)S(1)}, u32[]{:S(2)}, u32[]{:S(2)}) collective-permute-start(s32[1,2]{1,0:T(1,128)S(1)} %bitcast.200), channel_id=1, source_target_pairs={{0,8},{4,12},{8,0},{12,4},{16,24},{20,28},{24,16},{28,20},{1,9},{5... | collective-permute-start | bytes 32 | tf_op jit(solution)/shard_map/ppermute | solution.py:32
  32.1 3.0 %collective-permute-start.4 = (s32[1,2]{1,0:T(1,128)S(1)}, s32[1,2]{1,0:T(1,128)S(1)}, u32[]{:S(2)}, u32[]{:S(2)}) collective-permute-start(s32[1,2]{1,0:T(1,128)S(1)} %bitcast.199), channel_id=1, source_target_pairs={{0,12},{4,8},{8,4},{12,0},{16,28},{20,24},{24,20},{28,16},{1,13},{... | collective-permute-start | bytes 32 | tf_op jit(solution)/shard_map/ppermute | solution.py:32
  35.0 3.6 %collective-permute-start.5 = (s32[1,2]{1,0:T(1,128)S(1)}, s32[1,2]{1,0:T(1,128)S(1)}, u32[]{:S(2)}, u32[]{:S(2)}) collective-permute-start(s32[1,2]{1,0:T(1,128)S(1)} %bitcast.198), channel_id=1, source_target_pairs={{0,16},{4,20},{8,24},{12,28},{16,0},{20,4},{24,8},{28,12},{1,17},{... | collective-permute-start | bytes 32 | tf_op jit(solution)/shard_map/ppermute | solution.py:32
  38.6 3.0 %collective-permute-start.6 = (s32[1,2]{1,0:T(1,128)S(1)}, s32[1,2]{1,0:T(1,128)S(1)}, u32[]{:S(2)}, u32[]{:S(2)}) collective-permute-start(s32[1,2]{1,0:T(1,128)S(1)} %bitcast.197), channel_id=1, source_target_pairs={{0,20},{4,16},{8,28},{12,24},{16,4},{20,0},{24,12},{28,8},{1,21},{... | collective-permute-start | bytes 32 | tf_op jit(solution)/shard_map/ppermute | solution.py:32
  42.4 5.0 %copy-start.20 = (f32[6,8,128]{2,1,0:T(8,128)S(1)}, f32[6,8,128]{2,1,0:T(8,128)}, u32[]{:S(2)}) copy-start(f32[6,8,128]{2,1,0:T(8,128)} %param.7) | copy-start | bytes 73732
  43.2 17.6 %all-to-all-start.1 = ((f32[8,2,8]{2,1,0:T(2,128)}), f32[8,2,8]{2,1,0:T(2,128)S(1)}, u32[]{:S(2)}, u32[]{:S(2)}) async-start(f32[8,2,8]{2,1,0:T(2,128)} %bitcast.14), calls=%async_computation.1 | async-start | bytes 16384 | tf_op jit(solution)/shard_map/all_to_all | solution.py:92
  63.5 0.8 copy-start.5
  63.5 0.8 copy-start.4
  63.5 0.8 copy-start.3
  68.9 34.0 %collective-permute-start.10 = (f32[6,32,128]{2,1,0:T(8,128)S(1)}, f32[6,32,128]{2,1,0:T(8,128)}, u32[]{:S(2)}, u32[]{:S(2)}) collective-permute-start(f32[6,32,128]{2,1,0:T(8,128)S(1)} %get-tuple-element.13), channel_id=1, source_target_pairs={{0,4},{4,8},{8,12},{12,16},{16,20},{20,24},{24,28},{1,5},{5,9},{9,... | collective-permute-start | bytes 294920 | tf_op jit(solution)/shard_map/ppermute | solution.py:44
  70.8 32.1 %collective-permute-start.9 = (f32[6,32,128]{2,1,0:T(8,128)S(1)}, f32[6,32,128]{2,1,0:T(8,128)}, u32[]{:S(2)}, u32[]{:S(2)}) collective-permute-start(f32[6,32,128]{2,1,0:T(8,128)S(1)} %get-tuple-element.13), channel_id=1, source_target_pairs={{4,0},{8,4},{12,8},{16,12},{20,16},{24,20},{28,24},{5,1},{9,5},{13... | collective-permute-start | bytes 294920 | tf_op jit(solution)/shard_map/ppermute | solution.py:45
  80.3 11.4 %all-to-all-start.2 = ((f32[8,2,8]{2,1,0:T(2,128)}), f32[8,2,8]{2,1,0:T(2,128)S(1)}, u32[]{:S(2)}, u32[]{:S(2)}) async-start(f32[8,2,8]{2,1,0:T(2,128)} %broadcast_multiply_fusion.3), calls=%async_computation.2 | async-start | bytes 16384 | tf_op jit(solution)/shard_map/all_to_all | solution.py:86
  87.6 4.1 %copy-start.29 = (s32[16]{0:T(128)S(1)}, s32[16]{0:T(128)}, u32[]{:S(2)}) copy-start(s32[16]{0:T(128)} %copy-done.28) | copy-start | bytes 196
  93.1 8.0 %all-to-all-start.3 = ((f32[8,2,8]{2,1,0:T(2,128)}), f32[8,2,8]{2,1,0:T(2,128)S(1)}, u32[]{:S(2)}, u32[]{:S(2)}) async-start(f32[8,2,8]{2,1,0:T(2,128)} %bitcast.28), calls=%async_computation.3 | async-start | bytes 16384 | tf_op jit(solution)/shard_map/all_to_all | solution.py:92
  103.0 0.7 copy-start.17
  103.0 0.8 copy-start.11
  103.0 0.8 copy-start.10
  103.0 0.8 copy-start.9
  108.4 32.1 %collective-permute-start.12 = (f32[6,32,128]{2,1,0:T(8,128)S(1)}, f32[6,32,128]{2,1,0:T(8,128)}, u32[]{:S(2)}, u32[]{:S(2)}) collective-permute-start(f32[6,32,128]{2,1,0:T(8,128)S(1)} %multiply_subtract_fusion.1), channel_id=1, source_target_pairs={{0,4},{4,8},{8,12},{12,16},{16,20},{20,24},{24,28},{1,5},{5,9},{9,... | collective-permute-start | bytes 294920 | tf_op jit(solution)/shard_map/ppermute | solution.py:44
  110.7 29.7 %collective-permute-start.11 = (f32[6,32,128]{2,1,0:T(8,128)S(1)}, f32[6,32,128]{2,1,0:T(8,128)}, u32[]{:S(2)}, u32[]{:S(2)}) collective-permute-start(f32[6,32,128]{2,1,0:T(8,128)S(1)} %multiply_subtract_fusion.1), channel_id=1, source_target_pairs={{4,0},{8,4},{12,8},{16,12},{20,16},{24,20},{28,24},{5,1},{9,5},{13... | collective-permute-start | bytes 294920 | tf_op jit(solution)/shard_map/ppermute | solution.py:45
  119.7 9.4 %all-to-all-start.4 = ((f32[8,2,8]{2,1,0:T(2,128)}), f32[8,2,8]{2,1,0:T(2,128)S(1)}, u32[]{:S(2)}, u32[]{:S(2)}) async-start(f32[8,2,8]{2,1,0:T(2,128)} %broadcast_multiply_fusion.2), calls=%async_computation.4 | async-start | bytes 16384 | tf_op jit(solution)/shard_map/all_to_all | solution.py:86
  124.9 4.1 %copy-start.30 = (s32[16]{0:T(128)S(1)}, s32[16]{0:T(128)}, u32[]{:S(2)}) copy-start(s32[16]{0:T(128)} %copy-done.28) | copy-start | bytes 196
  130.5 8.2 %all-to-all-start.5 = ((f32[8,2,8]{2,1,0:T(2,128)}), f32[8,2,8]{2,1,0:T(2,128)S(1)}, u32[]{:S(2)}, u32[]{:S(2)}) async-start(f32[8,2,8]{2,1,0:T(2,128)} %bitcast.42), calls=%async_computation.5 | async-start | bytes 16384 | tf_op jit(solution)/shard_map/all_to_all | solution.py:92
  140.5 0.7 copy-start.18
  140.5 0.8 copy-start.14
  140.5 0.8 copy-start.13
  140.5 0.8 copy-start.12
  145.9 32.7 %collective-permute-start.14 = (f32[6,32,128]{2,1,0:T(8,128)S(1)}, f32[6,32,128]{2,1,0:T(8,128)}, u32[]{:S(2)}, u32[]{:S(2)}) collective-permute-start(f32[6,32,128]{2,1,0:T(8,128)S(1)} %multiply_subtract_fusion), channel_id=1, source_target_pairs={{0,4},{4,8},{8,12},{12,16},{16,20},{20,24},{24,28},{1,5},{5,9},{9,... | collective-permute-start | bytes 294920 | tf_op jit(solution)/shard_map/ppermute | solution.py:44
  148.2 30.3 %collective-permute-start.13 = (f32[6,32,128]{2,1,0:T(8,128)S(1)}, f32[6,32,128]{2,1,0:T(8,128)}, u32[]{:S(2)}, u32[]{:S(2)}) collective-permute-start(f32[6,32,128]{2,1,0:T(8,128)S(1)} %multiply_subtract_fusion), channel_id=1, source_target_pairs={{4,0},{8,4},{12,8},{16,12},{20,16},{24,20},{28,24},{5,1},{9,5},{13... | collective-permute-start | bytes 294920 | tf_op jit(solution)/shard_map/ppermute | solution.py:45
  157.1 9.4 %all-to-all-start.6 = ((f32[8,2,8]{2,1,0:T(2,128)}), f32[8,2,8]{2,1,0:T(2,128)S(1)}, u32[]{:S(2)}, u32[]{:S(2)}) async-start(f32[8,2,8]{2,1,0:T(2,128)} %broadcast_multiply_fusion.1), calls=%async_computation.6 | async-start | bytes 16384 | tf_op jit(solution)/shard_map/all_to_all | solution.py:86
  162.4 4.1 %copy-start.31 = (s32[16]{0:T(128)S(1)}, s32[16]{0:T(128)}, u32[]{:S(2)}) copy-start(s32[16]{0:T(128)} %copy-done.28) | copy-start | bytes 196
  167.9 8.0 %all-to-all-start.7 = ((f32[8,2,8]{2,1,0:T(2,128)}), f32[8,2,8]{2,1,0:T(2,128)S(1)}, u32[]{:S(2)}, u32[]{:S(2)}) async-start(f32[8,2,8]{2,1,0:T(2,128)} %bitcast.56), calls=%async_computation.7 | async-start | bytes 16384 | tf_op jit(solution)/shard_map/all_to_all | solution.py:92
  177.1 1.5 copy-start.2
  177.2 1.5 copy-start.24
  178.6 0.7 copy-start.16
  178.6 0.8 copy-start.8
  178.6 0.8 copy-start.7
  178.6 0.8 copy-start.6
  (7 other events, 4.7 us)
